TPU v7x, 32 devices: a whole 2x2x4 slice. The times are simulated.
32 devices in a mesh: groups: 2 (over y), ctx: 4 (over z), tp: 4 (over x, core).
Axes of the slice: x: 2, y: 2, z: 4, core: 2. Of those that a mesh axis runs over, the one named last changes fastest.
Arguments:
- hidden: bfloat16 [1024, 8192], P(('groups', 'ctx'), 'tp'), parts along dimension 0, may hold values from -6 to 6
- base_query_rows: bfloat16 [1024, 8192], P(('groups', 'ctx'), 'tp'), parts along dimension 0, may hold values from -60 to 60
- base_key_rows: bfloat16 [1024, 1024], P(('groups', 'ctx'), 'tp'), parts along dimension 0, may hold values from -60 to 60
- base_value_rows: bfloat16 [1024, 1024], P(('groups', 'ctx'), 'tp'), parts along dimension 0, may hold values from -6 to 6
- stored_block_order: int32 [16], P('groups'), parts along dimension 0, may hold values from 0 to 7, each once
- version: int32 [8], P('groups'), parts along dimension 0, may hold values from 0 to 3
- publisher: int32 [2], P('groups'), parts along dimension 0, may hold values from 0 to 3
- adapter_down_weight: bfloat16 [4, 4, 192, 8192], P('ctx', None, None, 'tp'), may hold values from -0.0625 to 0.0625
- adapter_up_query: bfloat16 [4, 4, 64, 8192], P('ctx', None, None, 'tp'), may hold values from -0.75 to 0.75
- adapter_up_key_value: bfloat16 [4, 4, 2, 64, 1024], P('ctx', None, None, None, 'tp'), may hold values from -0.75 to 0.75
- output_down_weight: bfloat16 [4, 4, 64, 8192], P('ctx', None, None, 'tp'), may hold values from -0.1875 to 0.1875
- output_up_weight: bfloat16 [4, 4, 64, 8192], P('ctx', None, None, 'tp'), may hold values from -0.75 to 0.75
Outputs:
- attended: bfloat16 [1024, 8192], P(('groups', 'ctx'), 'tp'), parts along dimension 0
- adapted: bfloat16 [1024, 8192], P(('groups', 'ctx'), 'tp'), parts along dimension 0
There are 2 independent parts, one for each index of `groups`. A program takes and returns all parts, laid end to end along the dimension named above; an argument that names none is the same for every part. Nothing has to cross between parts.
Inputs may be any that keep to these rules, and one draw needn't show every extreme that they name: `stored_block_order`: each half-block of the prompt is stored exactly once.
All inputs are finite; a program needn't handle non-finite values.
Results may differ from a plain program's by a relative error of at most 0.015.
The roundings to bfloat16 on the way count: a program that leaves them out, or rounds other values in their place, can miss the bound.
Values may be sent and summed in bfloat16 or wider, within the bound.
No kernel may reach another device: no remote copies, remote signals or barrier semaphores. Data moves between devices by JAX's collectives and lax.ppermute only.
A program may use at most 64 MiB of HBM per device.

v0:
```python
import jax
import jax.numpy as jnp
from jax import lax
from jax.sharding import PartitionSpec as P

HEAD_SIZE = 128
ADAPTER_RANK = 64
NEG_BIG = -1e30


def spread(value, axis, source):
    kept = jnp.where(lax.axis_index(axis) == source, value, 0).astype(value.dtype)
    return lax.psum(kept, axis)


def from_behind(value, axis, steps):
    count = lax.axis_size(axis)
    pairs = [(source, (source + steps) % count) for source in range(count)]
    return lax.ppermute(value, axis, pairs)


def apply_rotation(values, token_index_list):
    half_dim = values.shape[-1] // 2
    frequency = 500000.0 ** (-(jnp.arange(half_dim, dtype=jnp.float32) * 2.0) / values.shape[-1])
    angles = token_index_list.astype(jnp.float32)[:, None] * frequency[None, :]
    cosine = jnp.cos(angles)[:, None, :]
    sine_part = jnp.sin(angles)[:, None, :]
    first_half = values[..., :half_dim]
    second_half = values[..., half_dim:]
    return jnp.concatenate(
        [
            first_half * cosine - second_half * sine_part,
            second_half * cosine + first_half * sine_part,
        ],
        axis=-1,
    )


def pick_slot_version(stored, chosen_version):
    return lax.dynamic_index_in_dim(stored[0], chosen_version, 0, keepdims=False)


def token_positions(stored_block_order, first_row, row_count, half_rows):
    flat_index = first_row + jnp.arange(row_count, dtype=jnp.int32)
    block_index = flat_index // half_rows
    matches = (
        block_index[:, None] == jnp.arange(stored_block_order.shape[0], dtype=jnp.int32)[None, :]
    )
    stored_block = jnp.sum(jnp.where(matches, stored_block_order[None, :], 0), axis=1)
    return stored_block * half_rows + flat_index % half_rows


def attend_block(
    softmax_state, adapted_queries, query_pos, adapted_key_rows, adapted_value_rows, key_pos
):
    running_max, totals, accum = softmax_state
    scores = jnp.einsum(
        "tkgd,skd->kgts", adapted_queries, adapted_key_rows, preferred_element_type=jnp.float32
    ) * HEAD_SIZE ** (-0.5)
    visible = (key_pos[None, :] <= query_pos[:, None])[None, None]
    scores = jnp.where(visible, scores, NEG_BIG)
    new_max = jnp.maximum(running_max, jnp.max(scores, axis=-1))
    rescale = jnp.exp(running_max - new_max)
    raw_scores = jnp.where(visible, jnp.exp(scores - new_max[..., None]), 0.0)
    totals = totals * rescale + jnp.sum(raw_scores, axis=-1)
    accum = accum * rescale[..., None] + jnp.einsum(
        "kgts,skd->kgtd",
        raw_scores.astype(jnp.bfloat16),
        adapted_value_rows,
        preferred_element_type=jnp.float32,
    )
    return (new_max, totals, accum)


def shards(
    hidden,
    base_query_rows,
    base_key_rows,
    base_value_rows,
    stored_block_order,
    version,
    publisher,
    adapter_down_weight,
    adapter_up_query,
    adapter_up_key_value,
    output_down_weight,
    output_up_weight,
):
    source_block = publisher[0]
    chosen_version = lax.dynamic_index_in_dim(version, source_block, 0, keepdims=False)
    down_output, up_query, up_pair, outer_down, outer_up = (
        spread(pick_slot_version(adapter_down_weight, chosen_version), "ctx", source_block),
        spread(pick_slot_version(adapter_up_query, chosen_version), "ctx", source_block),
        spread(pick_slot_version(adapter_up_key_value, chosen_version), "ctx", source_block),
        spread(pick_slot_version(output_down_weight, chosen_version), "ctx", source_block),
        spread(pick_slot_version(output_up_weight, chosen_version), "ctx", source_block),
    )
    partial_value = lax.dot_general(
        hidden, down_output, (((1,), (1,)), ((), ())), preferred_element_type=jnp.float32
    )
    rank_projection = lax.psum(partial_value, "tp").astype(jnp.bfloat16)
    local_rows = hidden.shape[0]
    half_rows = local_rows // 2
    cycle_size = lax.axis_size("ctx")
    own_index = lax.axis_index("ctx")
    query_pos = token_positions(stored_block_order, own_index * local_rows, local_rows, half_rows)
    local_heads = base_query_rows.shape[1] // HEAD_SIZE
    local_groups = base_key_rows.shape[1] // HEAD_SIZE
    query_group_size = local_heads // local_groups
    adapted_queries = base_query_rows.astype(jnp.float32) + jnp.dot(
        rank_projection[:, :ADAPTER_RANK], up_query, preferred_element_type=jnp.float32
    )
    adapted_queries = apply_rotation(
        adapted_queries.reshape(local_rows, local_heads, HEAD_SIZE), query_pos
    ).astype(jnp.bfloat16)
    adapted_queries = adapted_queries.reshape(local_rows, local_groups, query_group_size, HEAD_SIZE)
    adapted_key_rows = base_key_rows.astype(jnp.float32) + jnp.dot(
        rank_projection[:, ADAPTER_RANK : 2 * ADAPTER_RANK],
        up_pair[0],
        preferred_element_type=jnp.float32,
    )
    adapted_key_rows = apply_rotation(
        adapted_key_rows.reshape(local_rows, local_groups, HEAD_SIZE), query_pos
    ).astype(jnp.bfloat16)
    adapted_value_rows = base_value_rows.astype(jnp.float32) + jnp.dot(
        rank_projection[:, 2 * ADAPTER_RANK :], up_pair[1], preferred_element_type=jnp.float32
    )
    adapted_value_rows = adapted_value_rows.astype(jnp.bfloat16).reshape(
        local_rows, local_groups, HEAD_SIZE
    )
    empty_state = (
        jnp.full((local_groups, query_group_size, local_rows), NEG_BIG, jnp.float32),
        jnp.zeros((local_groups, query_group_size, local_rows), jnp.float32),
        jnp.zeros((local_groups, query_group_size, local_rows, HEAD_SIZE), jnp.float32),
    )
    first_state = attend_block(
        empty_state, adapted_queries, query_pos, adapted_key_rows, adapted_value_rows, query_pos
    )

    def cycle_turn(turn, carried):
        moving_keys, moving_values, softmax_state = carried
        moving_keys, moving_values = from_behind((moving_keys, moving_values), "ctx", 1)
        sender = (own_index - turn - 1) % cycle_size
        key_pos = token_positions(stored_block_order, sender * local_rows, local_rows, half_rows)
        return (
            moving_keys,
            moving_values,
            attend_block(
                softmax_state, adapted_queries, query_pos, moving_keys, moving_values, key_pos
            ),
        )

    final_state = lax.fori_loop(
        0, cycle_size - 1, cycle_turn, (adapted_key_rows, adapted_value_rows, first_state)
    )[2]
    running_max, totals, accum = final_state
    attended = (
        jnp.transpose(accum / totals[..., None], (2, 0, 1, 3))
        .reshape(local_rows, local_heads * HEAD_SIZE)
        .astype(jnp.bfloat16)
    )
    out_partial = lax.dot_general(
        attended, outer_down, (((1,), (1,)), ((), ())), preferred_element_type=jnp.float32
    )
    out_low = lax.psum(out_partial.astype(jnp.bfloat16), "tp")
    adapted = jnp.dot(out_low, outer_up, preferred_element_type=jnp.float32).astype(jnp.bfloat16)
    return (attended, adapted)


def solution(mesh):
    placed = (
        P(("groups", "ctx"), "tp"),
        P(("groups", "ctx"), "tp"),
        P(("groups", "ctx"), "tp"),
        P(("groups", "ctx"), "tp"),
        P("groups"),
        P("groups"),
        P("groups"),
        P("ctx", None, None, "tp"),
        P("ctx", None, None, "tp"),
        P("ctx", None, None, None, "tp"),
        P("ctx", None, None, "tp"),
        P("ctx", None, None, "tp"),
    )
    return jax.shard_map(
        shards,
        mesh=mesh,
        in_specs=placed,
        out_specs=(P(("groups", "ctx"), "tp"), P(("groups", "ctx"), "tp")),
        check_vma=False,
    )
```

profile of v0, /device:TPU:0, one launch (start us, length us, event | category | flops | bytes accessed | tf_op | source)
XLA Modules:
  0.0 154.0 jit_solution(17024715240164693517)
XLA Ops:
  7.9 1.2 dynamic_slice.22
  11.1 2.1 %select_bitcast_fusion = bf16[192,2048]{1,0:T(8,128)(2,1)} fusion(bf16[1,4,192,2048]{3,2,1,0:T(8,128)(2,1)} %param.21, s32[]{:T(128)S(6)} %select_n.191, pred[]{:T(512)S(6)} %eq.79), kind=kLoop, calls=%fused_computation.43 | loop fusion | flops 393216 | bytes 1572869 | tf_op jit(solution)/shard_map/jit(_where)/select_n | solution.py:12
  13.3 1.7 %select_bitcast_fusion.3 = bf16[64,2048]{1,0:T(8,128)(2,1)} fusion(bf16[1,4,64,2048]{3,2,1,0:T(8,128)(2,1)} %param.22, s32[]{:T(128)S(6)} %select_n.191, pred[]{:T(512)S(6)} %eq.79), kind=kLoop, calls=%fused_computation.52 | loop fusion | flops 131072 | bytes 524293 | tf_op jit(solution)/shard_map/jit(_where)/select_n | solution.py:12
  15.0 1.5 select_bitcast_fusion.4
  16.5 1.9 %select_bitcast_fusion.1 = (bf16[64,2048]{1,0:T(8,128)(2,1)}, bf16[64,2048]{1,0:T(8,128)(2,1)}) fusion(bf16[1,4,64,2048]{3,2,1,0:T(8,128)(2,1)} %param.25, s32[]{:T(128)S(6)} %select_n.191, pred[]{:T(512)S(6)} %eq.79, bf16[1,4,64,2048]{3,2,1,0:T(8,128)(2,1)} %param.24), kind=kLoop, calls=%fused_computation.50 | loop fusion | flops 262144 | bytes 1048581 | tf_op jit(solution)/shard_map/jit(_where)/select_n | solution.py:12
  18.9 73.7 %all-reduce.3.cloned.1.call-done = (bf16[2,64,256]{2,1,0:T(8,128)(2,1)}, bf16[192,2048]{1,0:T(8,128)(2,1)}, bf16[64,2048]{1,0:T(8,128)(2,1)}, bf16[64,2048]{1,0:T(8,128)(2,1)}, bf16[64,2048]{1,0:T(8,128)(2,1)}) async-done(((bf16[2,64,256]{2,1,0:T(8,128)(2,1)}, bf16[192,2048]{1,0:T(8,128)(2,1)}, bf16[64,2048]{1,0:T(8,128)(2,1)}, bf16[64,2048]{1,0:T(8,128)(2,1)}, bf16[64,2048]{1,0:T(8,128)(2,1)}), ...) | async-done | bytes 1638416 | tf_op jit(solution)/shard_map/psum | solution.py:13
  92.6 1.5 convolution_bitcast_fusion
  94.1 11.6 %psum.50 = bf16[128,192]{0,1:T(8,128)(2,1)S(1)} all-reduce(f32[128,192]{0,1:T(8,128)S(1)} %convolution_bitcast_fusion), channel_id=1, replica_groups=mesh['groups'=2,'ctx'=4,'tp'=4] {'tp'}, use_global_device_ids=true, to_apply=%region_1.2 | all-reduce | flops 24576 | bytes 147456 | tf_op jit(solution)/shard_map/psum | solution.py:101
  105.8 1.0 fusion.15
  106.8 1.3 fusion.12
  108.3 0.5 subtract_convert_fusion
  110.6 0.5 convolution_add_fusion.2
  111.2 23.1 %while.24 = (s32[]{:T(128)}, bf16[128,2,128]{2,0,1:T(8,128)(2,1)S(1)}, bf16[128,2,128]{2,0,1:T(8,128)(2,1)S(1)}, f32[2,8,128]{2,1,0:T(8,128)S(1)}, f32[2,8,128]{...) while((s32[]{:T(128)}, ...), condition=%wide.region_11.12_spmd, body=%wide.region_7.11_spmd.sunk | while | flops 137128592 | bytes 6885278 | solution.py:153
  111.2 0.5 collective-permute-start
  111.7 2.0 %collective-permute-start.1 = (bf16[128,2,128]{2,0,1:T(8,128)(2,1)S(1)}, bf16[128,2,128]{2,0,1:T(8,128)(2,1)S(1)}, u32[]{:S(2)}, u32[]{:S(2)}) collective-permute-start(bf16[128,2,128]{2,0,1:T(8,128)(2,1)S(1)} %get-tuple-element.440), channel_id=1, source_target_pairs={{0,4},{4,8},{8,12},{12,0},{1,5},{5,9},{9,13},{13,1},{2,6},{6,10},{... | collective-permute-start | bytes 196616 | tf_op jit(solution)/shard_map/while/body/eval_jaxpr/ppermute | solution.py:19
  113.9 3.9 %collective-permute-done = bf16[128,2,128]{2,0,1:T(8,128)(2,1)S(1)} collective-permute-done((bf16[128,2,128]{2,0,1:T(8,128)(2,1)S(1)}, bf16[128,2,128]{2,0,1:T(8,128)(2,1)S(1)}, u32[]{:S(2)}, u32[]{:S(2)}) %collective-permute-start) | collective-permute-done | bytes 65568 | tf_op jit(solution)/shard_map/while/body/eval_jaxpr/ppermute | solution.py:19
  118.5 0.7 convolution_add_fusion.6
  119.6 5.7 %collective-permute-done = bf16[128,2,128]{2,0,1:T(8,128)(2,1)S(1)} collective-permute-done((bf16[128,2,128]{2,0,1:T(8,128)(2,1)S(1)}, bf16[128,2,128]{2,0,1:T(8,128)(2,1)S(1)}, u32[]{:S(2)}, u32[]{:S(2)}) %collective-permute-start) | collective-permute-done | bytes 65568 | tf_op jit(solution)/shard_map/while/body/eval_jaxpr/ppermute | solution.py:19
  126.0 0.7 convolution_add_fusion.6
  127.1 5.8 %collective-permute-done = bf16[128,2,128]{2,0,1:T(8,128)(2,1)S(1)} collective-permute-done((bf16[128,2,128]{2,0,1:T(8,128)(2,1)S(1)}, bf16[128,2,128]{2,0,1:T(8,128)(2,1)S(1)}, u32[]{:S(2)}, u32[]{:S(2)}) %collective-permute-start) | collective-permute-done | bytes 65568 | tf_op jit(solution)/shard_map/while/body/eval_jaxpr/ppermute | solution.py:19
  133.6 0.7 convolution_add_fusion.6
  134.6 0.3 copy.31
  135.5 10.6 %psum.54 = bf16[128,64]{1,0:T(8,128)(2,1)S(1)} all-reduce(bf16[128,64]{1,0:T(8,128)(2,1)S(1)} %convolution_convert_fusion.1), channel_id=1, replica_groups=mesh['groups'=2,'ctx'=4,'tp'=4] {'tp'}, use_global_device_ids=true, to_apply=%region_13.14 | all-reduce | flops 8192 | bytes 32768 | tf_op jit(solution)/shard_map/psum | solution.py:165
  146.1 1.1 convolution_convert_fusion
  (84 shorter events, 6.3 us)
Async XLA Ops:
  7.2 85.5 %copy-start = (bf16[128,2048]{1,0:T(8,128)(2,1)S(1)}, bf16[128,2048]{1,0:T(8,128)(2,1)}, u32[]{:S(2)}) copy-start(bf16[128,2048]{1,0:T(8,128)(2,1)} %param.14) | copy-start | bytes 1572868
  7.2 11.2 %copy-start.8 = (s32[8]{0:T(128)S(1)}, s32[8]{0:T(128)}, u32[]{:S(2)}) copy-start(s32[8]{0:T(128)} %param.18) | copy-start | bytes 100
  7.2 85.4 %all-reduce.3.cloned.1.call-start = ((), (), s32[]{:S(2)}) async-start(), calls=%async_computation | async-start | bytes 3276800 | tf_op jit(solution)/shard_map/psum | solution.py:13
  11.1 94.6 %copy-start.6 = (bf16[128,256]{1,0:T(8,128)(2,1)S(1)}, bf16[128,256]{1,0:T(8,128)(2,1)}, u32[]{:S(2)}) copy-start(bf16[128,256]{1,0:T(8,128)(2,1)} %param.17) | copy-start | bytes 196612
  13.3 93.5 %copy-start.2 = (bf16[128,2048]{1,0:T(8,128)(2,1)S(1)}, bf16[128,2048]{1,0:T(8,128)(2,1)}, u32[]{:S(2)}) copy-start(bf16[128,2048]{1,0:T(8,128)(2,1)} %param.15) | copy-start | bytes 1572868
  108.3 0.9 copy-start.5
  108.3 0.9 copy-start.7
  111.2 6.6 %collective-permute-start = (bf16[128,2,128]{2,0,1:T(8,128)(2,1)S(1)}, bf16[128,2,128]{2,0,1:T(8,128)(2,1)S(1)}, u32[]{:S(2)}, u32[]{:S(2)}) collective-permute-start(bf16[128,2,128]{2,0,1:T(8,128)(2,1)S(1)} %get-tuple-element.439), channel_id=1, source_target_pairs={{0,4},{4,8},{8,12},{12,0},{1,5},{5,9},{9,13},{13,1},{2,6},{6,10},{... | collective-permute-start | bytes 196616 | tf_op jit(solution)/shard_map/while/body/eval_jaxpr/ppermute | solution.py:19
  111.7 6.8 %collective-permute-start.1 = (bf16[128,2,128]{2,0,1:T(8,128)(2,1)S(1)}, bf16[128,2,128]{2,0,1:T(8,128)(2,1)S(1)}, u32[]{:S(2)}, u32[]{:S(2)}) collective-permute-start(bf16[128,2,128]{2,0,1:T(8,128)(2,1)S(1)} %get-tuple-element.440), channel_id=1, source_target_pairs={{0,4},{4,8},{8,12},{12,0},{1,5},{5,9},{9,13},{13,1},{2,6},{6,10},{... | collective-permute-start | bytes 196616 | tf_op jit(solution)/shard_map/while/body/eval_jaxpr/ppermute | solution.py:19
  119.2 6.1 %collective-permute-start = (bf16[128,2,128]{2,0,1:T(8,128)(2,1)S(1)}, bf16[128,2,128]{2,0,1:T(8,128)(2,1)S(1)}, u32[]{:S(2)}, u32[]{:S(2)}) collective-permute-start(bf16[128,2,128]{2,0,1:T(8,128)(2,1)S(1)} %get-tuple-element.439), channel_id=1, source_target_pairs={{0,4},{4,8},{8,12},{12,0},{1,5},{5,9},{9,13},{13,1},{2,6},{6,10},{... | collective-permute-start | bytes 196616 | tf_op jit(solution)/shard_map/while/body/eval_jaxpr/ppermute | solution.py:19
  119.3 6.8 %collective-permute-start.1 = (bf16[128,2,128]{2,0,1:T(8,128)(2,1)S(1)}, bf16[128,2,128]{2,0,1:T(8,128)(2,1)S(1)}, u32[]{:S(2)}, u32[]{:S(2)}) collective-permute-start(bf16[128,2,128]{2,0,1:T(8,128)(2,1)S(1)} %get-tuple-element.440), channel_id=1, source_target_pairs={{0,4},{4,8},{8,12},{12,0},{1,5},{5,9},{9,13},{13,1},{2,6},{6,10},{... | collective-permute-start | bytes 196616 | tf_op jit(solution)/shard_map/while/body/eval_jaxpr/ppermute | solution.py:19
  126.7 6.1 %collective-permute-start = (bf16[128,2,128]{2,0,1:T(8,128)(2,1)S(1)}, bf16[128,2,128]{2,0,1:T(8,128)(2,1)S(1)}, u32[]{:S(2)}, u32[]{:S(2)}) collective-permute-start(bf16[128,2,128]{2,0,1:T(8,128)(2,1)S(1)} %get-tuple-element.439), channel_id=1, source_target_pairs={{0,4},{4,8},{8,12},{12,0},{1,5},{5,9},{9,13},{13,1},{2,6},{6,10},{... | collective-permute-start | bytes 196616 | tf_op jit(solution)/shard_map/while/body/eval_jaxpr/ppermute | solution.py:19
  126.8 6.8 %collective-permute-start.1 = (bf16[128,2,128]{2,0,1:T(8,128)(2,1)S(1)}, bf16[128,2,128]{2,0,1:T(8,128)(2,1)S(1)}, u32[]{:S(2)}, u32[]{:S(2)}) collective-permute-start(bf16[128,2,128]{2,0,1:T(8,128)(2,1)S(1)} %get-tuple-element.440), channel_id=1, source_target_pairs={{0,4},{4,8},{8,12},{12,0},{1,5},{5,9},{9,13},{13,1},{2,6},{6,10},{... | collective-permute-start | bytes 196616 | tf_op jit(solution)/shard_map/while/body/eval_jaxpr/ppermute | solution.py:19
  134.3 1.0 copy-start.4
  134.3 11.8 %copy-start.3 = (bf16[64,2048]{1,0:T(8,128)(2,1)S(1)}, bf16[64,2048]{1,0:T(8,128)(2,1)}, u32[]{:S(2)}) copy-start(bf16[64,2048]{1,0:T(8,128)(2,1)} %get-tuple-element.332) | copy-start | bytes 786436
  135.1 12.0 %copy-start.1 = (bf16[16,8,16,128]{3,1,2,0:T(8,128)(2,1)}, bf16[16,8,16,128]{3,1,2,0:T(8,128)(2,1)S(1)}, u32[]{:S(2)}) copy-start(bf16[16,8,16,128]{3,1,2,0:T(8,128)(2,1)S(1)} %copy.53) | copy-start | bytes 1572868
Sparse Core Ops, SparseCore 0:
  18.5 74.1 all-reduce.2
where the time goes:
time: 155 us; the launch traced here: 154 us
  waiting for transfers between devices  89.5 us (58%)
  blocking collectives  22.2 us (14%)
  between operations  17 us (11%)
  other arithmetic  10.5 us (7%)
  matrix products  9.11 us (6%)
  starting transfers between devices  2.9 us (2%)
  local copies, waits for them, and re-layouts  2.65 us (2%)
    psum x1, waiting for transfers between devices, spread(): return lax.psum(kept, axis)  73.7 us
    ppermute x6, waiting for transfers between devices, from_behind(): return lax.ppermute(value, axis, pairs)  15.7 us
    psum x1, blocking collectives, shards(): rank_projection = lax.psum(partial_value, 'tp').astype(jnp.bfloat16)  11.6 us
    psum x1, blocking collectives, shards(): out_low = lax.psum(out_partial.astype(jnp.bfloat16), 'tp')  10.6 us
    select_n x4, other arithmetic, spread(): jnp.where(lax.axis_index(axis) == source, value, 0).astype(value.dtype)  7.19 us
  transfers between devices with their start and end apart: 7, of which 7 were waited for; matrix products, arithmetic and copies ran while one was open for 2% of the time, Pallas kernels for 0%

commit v1 on v0

--- a/solution.py
+++ b/solution.py
@@ -98,7 +98,7 @@
     partial_value = lax.dot_general(
         hidden, down_output, (((1,), (1,)), ((), ())), preferred_element_type=jnp.float32
     )
-    rank_projection = lax.psum(partial_value, "tp").astype(jnp.bfloat16)
+    rank_projection = jnp.sum(lax.all_gather(partial_value, "tp"), axis=0).astype(jnp.bfloat16)
     local_rows = hidden.shape[0]
     half_rows = local_rows // 2
     cycle_size = lax.axis_size("ctx")

time: 155 us -> 148 us (0.955)
  blocking collectives: 22.2 us -> 16.6 us
  matrix products: 9.11 us -> 7.48 us
    psum x1 -> x0, blocking collectives: 11.6 us -> none  [shards(): rank_projection = lax.psum(partial_value, 'tp').astype(jnp.bfloat16)]
    all_gather x0 -> x1, blocking collectives: none -> 6.44 us  [shards(): lax.all_gather(partial_value, 'tp')]
where the time goes in v1:
time: 148 us; the launch traced here: 147 us
  waiting for transfers between devices  90.3 us (61%)
  between operations  17 us (11%)
  blocking collectives  16.6 us (11%)
  other arithmetic  10.7 us (7%)
  matrix products  7.48 us (5%)
  local copies, waits for them, and re-layouts  2.79 us (2%)
  starting transfers between devices  2.36 us (2%)
    psum x1, waiting for transfers between devices, spread(): return lax.psum(kept, axis)  73.7 us
    ppermute x6, waiting for transfers between devices, from_behind(): return lax.ppermute(value, axis, pairs)  16.5 us
    psum x1, blocking collectives, shards(): out_low = lax.psum(out_partial.astype(jnp.bfloat16), 'tp')  10.1 us
    select_n x4, other arithmetic, spread(): jnp.where(lax.axis_index(axis) == source, value, 0).astype(value.dtype)  7.18 us
    all_gather x1, blocking collectives, shards(): lax.all_gather(partial_value, 'tp')  6.44 us
  transfers between devices with their start and end apart: 7, of which 7 were waited for; matrix products, arithmetic and copies ran while one was open for 2% of the time, Pallas kernels for 0%

profile of v1, /device:TPU:0, one launch (start us, length us, event | category | flops | bytes accessed | tf_op | source)
XLA Modules:
  0.0 147.4 jit_solution(2870052941076502465)
XLA Ops:
  7.9 1.2 dynamic_slice.22
  11.1 2.1 %select_bitcast_fusion = bf16[192,2048]{1,0:T(8,128)(2,1)} fusion(bf16[1,4,192,2048]{3,2,1,0:T(8,128)(2,1)} %param.21, s32[]{:T(128)S(6)} %select_n.191, pred[]{:T(512)S(6)} %eq.79), kind=kLoop, calls=%fused_computation.43 | loop fusion | flops 393216 | bytes 1572869 | tf_op jit(solution)/shard_map/jit(_where)/select_n | solution.py:12
  13.2 1.7 %select_bitcast_fusion.3 = bf16[64,2048]{1,0:T(8,128)(2,1)} fusion(bf16[1,4,64,2048]{3,2,1,0:T(8,128)(2,1)} %param.22, s32[]{:T(128)S(6)} %select_n.191, pred[]{:T(512)S(6)} %eq.79), kind=kLoop, calls=%fused_computation.52 | loop fusion | flops 131072 | bytes 524293 | tf_op jit(solution)/shard_map/jit(_where)/select_n | solution.py:12
  14.9 1.5 %select_bitcast_fusion.4 = bf16[2,64,256]{2,1,0:T(8,128)(2,1)} fusion(bf16[1,4,2,64,256]{4,3,2,1,0:T(8,128)(2,1)} %param.23, s32[]{:T(128)S(6)} %select_n.191, pred[]{:T(512)S(6)} %eq.79), kind=kLoop, calls=%fused_computation.61 | loop fusion | flops 32768 | bytes 131077 | tf_op jit(solution)/shard_map/jit(_where)/select_n | solution.py:12
  16.4 1.9 %select_bitcast_fusion.1 = (bf16[64,2048]{1,0:T(8,128)(2,1)}, bf16[64,2048]{1,0:T(8,128)(2,1)}) fusion(bf16[1,4,64,2048]{3,2,1,0:T(8,128)(2,1)} %param.25, s32[]{:T(128)S(6)} %select_n.191, pred[]{:T(512)S(6)} %eq.79, bf16[1,4,64,2048]{3,2,1,0:T(8,128)(2,1)} %param.24), kind=kLoop, calls=%fused_computation.50 | loop fusion | flops 262144 | bytes 1048581 | tf_op jit(solution)/shard_map/jit(_where)/select_n | solution.py:12
  18.9 73.7 %all-reduce.3.cloned.1.call-done = (bf16[2,64,256]{2,1,0:T(8,128)(2,1)}, bf16[192,2048]{1,0:T(8,128)(2,1)}, bf16[64,2048]{1,0:T(8,128)(2,1)}, bf16[64,2048]{1,0:T(8,128)(2,1)}, bf16[64,2048]{1,0:T(8,128)(2,1)}) async-done(((bf16[2,64,256]{2,1,0:T(8,128)(2,1)}, bf16[192,2048]{1,0:T(8,128)(2,1)}, bf16[64,2048]{1,0:T(8,128)(2,1)}, bf16[64,2048]{1,0:T(8,128)(2,1)}, bf16[64,2048]{1,0:T(8,128)(2,1)}), ...) | async-done | bytes 1638416 | tf_op jit(solution)/shard_map/psum | solution.py:13
  92.6 1.5 %convolution_bitcast_fusion = f32[128,192]{0,1:T(8,128)S(1)} fusion(bf16[192,2048]{1,0:T(8,128)(2,1)} %get-tuple-element.339, bf16[128,2048]{1,0:T(8,128)(2,1)S(1)} %copy-done), kind=kOutput, calls=%fused_computation.34 | convolution fusion | flops 100663296 | bytes 1409024 | tf_op jit(solution)/shard_map/dot_general | solution.py:98
  94.2 6.4 %all-gather = f32[512,192]{0,1:T(8,128)S(1)} all-gather(f32[128,192]{0,1:T(8,128)S(1)} %convolution_bitcast_fusion), channel_id=2, replica_groups=mesh['groups'=2,'ctx'=4,'tp'=4] {'tp'}, dimensions={0}, use_global_device_ids=true | all-gather | bytes 491520 | tf_op jit(solution)/shard_map/all_gather | solution.py:101
  101.3 0.3 fusion.12
  101.8 0.5 subtract_convert_fusion
  104.1 0.5 convolution_add_fusion.2
  104.7 23.4 %while.24 = (s32[]{:T(128)}, bf16[128,2,128]{2,0,1:T(8,128)(2,1)S(1)}, bf16[128,2,128]{2,0,1:T(8,128)(2,1)S(1)}, f32[2,8,128]{2,1,0:T(8,128)S(1)}, f32[2,8,128]{...) while((s32[]{:T(128)}, ...), condition=%wide.region_11.12_spmd, body=%wide.region_7.11_spmd.sunk | while | flops 137128592 | bytes 6885278 | solution.py:153
  104.7 0.7 collective-permute-start
  105.4 1.3 collective-permute-start.1
  106.9 4.6 %collective-permute-done = bf16[128,2,128]{2,0,1:T(8,128)(2,1)S(1)} collective-permute-done((bf16[128,2,128]{2,0,1:T(8,128)(2,1)S(1)}, bf16[128,2,128]{2,0,1:T(8,128)(2,1)S(1)}, u32[]{:S(2)}, u32[]{:S(2)}) %collective-permute-start) | collective-permute-done | bytes 65568 | tf_op jit(solution)/shard_map/while/body/eval_jaxpr/ppermute | solution.py:19
  112.3 0.7 convolution_add_fusion.6
  113.4 5.7 %collective-permute-done = bf16[128,2,128]{2,0,1:T(8,128)(2,1)S(1)} collective-permute-done((bf16[128,2,128]{2,0,1:T(8,128)(2,1)S(1)}, bf16[128,2,128]{2,0,1:T(8,128)(2,1)S(1)}, u32[]{:S(2)}, u32[]{:S(2)}) %collective-permute-start) | collective-permute-done | bytes 65568 | tf_op jit(solution)/shard_map/while/body/eval_jaxpr/ppermute | solution.py:19
  119.8 0.7 convolution_add_fusion.6
  120.9 5.8 %collective-permute-done = bf16[128,2,128]{2,0,1:T(8,128)(2,1)S(1)} collective-permute-done((bf16[128,2,128]{2,0,1:T(8,128)(2,1)S(1)}, bf16[128,2,128]{2,0,1:T(8,128)(2,1)S(1)}, u32[]{:S(2)}, u32[]{:S(2)}) %collective-permute-start) | collective-permute-done | bytes 65568 | tf_op jit(solution)/shard_map/while/body/eval_jaxpr/ppermute | solution.py:19
  127.4 0.7 convolution_add_fusion.6
  128.1 0.3 fusion.21
  128.4 0.3 copy.40
  129.3 10.1 %psum.46 = bf16[128,64]{0,1:T(8,128)(2,1)S(1)} all-reduce(bf16[128,64]{0,1:T(8,128)(2,1)S(1)} %convolution_convert_fusion.1), channel_id=1, replica_groups=mesh['groups'=2,'ctx'=4,'tp'=4] {'tp'}, use_global_device_ids=true, to_apply=%region_13.14 | all-reduce | flops 8192 | bytes 32768 | tf_op jit(solution)/shard_map/psum | solution.py:165
  139.4 1.1 convolution_convert_fusion
  (88 shorter events, 6.6 us)
Async XLA Ops:
  7.2 85.5 %copy-start = (bf16[128,2048]{1,0:T(8,128)(2,1)S(1)}, bf16[128,2048]{1,0:T(8,128)(2,1)}, u32[]{:S(2)}) copy-start(bf16[128,2048]{1,0:T(8,128)(2,1)} %param.14) | copy-start | bytes 1572868
  7.2 11.2 %copy-start.9 = (s32[8]{0:T(128)S(1)}, s32[8]{0:T(128)}, u32[]{:S(2)}) copy-start(s32[8]{0:T(128)} %param.18) | copy-start | bytes 100
  7.2 85.4 %all-reduce.3.cloned.1.call-start = ((), (), s32[]{:S(2)}) async-start(), calls=%async_computation | async-start | bytes 3276800 | tf_op jit(solution)/shard_map/psum | solution.py:13
  14.9 86.1 %copy-start.7 = (bf16[128,256]{1,0:T(8,128)(2,1)S(1)}, bf16[128,256]{1,0:T(8,128)(2,1)}, u32[]{:S(2)}) copy-start(bf16[128,256]{1,0:T(8,128)(2,1)} %param.17) | copy-start | bytes 196612
  16.4 84.9 %copy-start.2 = (bf16[128,2048]{1,0:T(8,128)(2,1)S(1)}, bf16[128,2048]{1,0:T(8,128)(2,1)}, u32[]{:S(2)}) copy-start(bf16[128,2048]{1,0:T(8,128)(2,1)} %param.15) | copy-start | bytes 1572868
  92.6 8.4 %copy-start.6 = (bf16[2,64,256]{2,1,0:T(8,128)(2,1)S(1)}, bf16[2,64,256]{2,1,0:T(8,128)(2,1)}, u32[]{:S(2)}) copy-start(bf16[2,64,256]{2,1,0:T(8,128)(2,1)} %get-tuple-element.338) | copy-start | bytes 196612
  92.6 8.7 %copy-start.5 = (bf16[64,2048]{1,0:T(8,128)(2,1)S(1)}, bf16[64,2048]{1,0:T(8,128)(2,1)}, u32[]{:S(2)}) copy-start(bf16[64,2048]{1,0:T(8,128)(2,1)} %get-tuple-element.340) | copy-start | bytes 786436
  101.8 0.9 copy-start.8
  104.7 6.8 %collective-permute-start = (bf16[128,2,128]{2,0,1:T(8,128)(2,1)S(1)}, bf16[128,2,128]{2,0,1:T(8,128)(2,1)S(1)}, u32[]{:S(2)}, u32[]{:S(2)}) collective-permute-start(bf16[128,2,128]{2,0,1:T(8,128)(2,1)S(1)} %get-tuple-element.449), channel_id=1, source_target_pairs={{0,4},{4,8},{8,12},{12,0},{1,5},{5,9},{9,13},{13,1},{2,6},{6,10},{... | collective-permute-start | bytes 196616 | tf_op jit(solution)/shard_map/while/body/eval_jaxpr/ppermute | solution.py:19
  105.4 6.9 %collective-permute-start.1 = (bf16[128,2,128]{2,0,1:T(8,128)(2,1)S(1)}, bf16[128,2,128]{2,0,1:T(8,128)(2,1)S(1)}, u32[]{:S(2)}, u32[]{:S(2)}) collective-permute-start(bf16[128,2,128]{2,0,1:T(8,128)(2,1)S(1)} %get-tuple-element.450), channel_id=1, source_target_pairs={{0,4},{4,8},{8,12},{12,0},{1,5},{5,9},{9,13},{13,1},{2,6},{6,10},{... | collective-permute-start | bytes 196616 | tf_op jit(solution)/shard_map/while/body/eval_jaxpr/ppermute | solution.py:19
  113.0 6.1 %collective-permute-start = (bf16[128,2,128]{2,0,1:T(8,128)(2,1)S(1)}, bf16[128,2,128]{2,0,1:T(8,128)(2,1)S(1)}, u32[]{:S(2)}, u32[]{:S(2)}) collective-permute-start(bf16[128,2,128]{2,0,1:T(8,128)(2,1)S(1)} %get-tuple-element.449), channel_id=1, source_target_pairs={{0,4},{4,8},{8,12},{12,0},{1,5},{5,9},{9,13},{13,1},{2,6},{6,10},{... | collective-permute-start | bytes 196616 | tf_op jit(solution)/shard_map/while/body/eval_jaxpr/ppermute | solution.py:19
  113.1 6.8 %collective-permute-start.1 = (bf16[128,2,128]{2,0,1:T(8,128)(2,1)S(1)}, bf16[128,2,128]{2,0,1:T(8,128)(2,1)S(1)}, u32[]{:S(2)}, u32[]{:S(2)}) collective-permute-start(bf16[128,2,128]{2,0,1:T(8,128)(2,1)S(1)} %get-tuple-element.450), channel_id=1, source_target_pairs={{0,4},{4,8},{8,12},{12,0},{1,5},{5,9},{9,13},{13,1},{2,6},{6,10},{... | collective-permute-start | bytes 196616 | tf_op jit(solution)/shard_map/while/body/eval_jaxpr/ppermute | solution.py:19
  120.5 6.1 %collective-permute-start = (bf16[128,2,128]{2,0,1:T(8,128)(2,1)S(1)}, bf16[128,2,128]{2,0,1:T(8,128)(2,1)S(1)}, u32[]{:S(2)}, u32[]{:S(2)}) collective-permute-start(bf16[128,2,128]{2,0,1:T(8,128)(2,1)S(1)} %get-tuple-element.449), channel_id=1, source_target_pairs={{0,4},{4,8},{8,12},{12,0},{1,5},{5,9},{9,13},{13,1},{2,6},{6,10},{... | collective-permute-start | bytes 196616 | tf_op jit(solution)/shard_map/while/body/eval_jaxpr/ppermute | solution.py:19
  120.6 6.8 %collective-permute-start.1 = (bf16[128,2,128]{2,0,1:T(8,128)(2,1)S(1)}, bf16[128,2,128]{2,0,1:T(8,128)(2,1)S(1)}, u32[]{:S(2)}, u32[]{:S(2)}) collective-permute-start(bf16[128,2,128]{2,0,1:T(8,128)(2,1)S(1)} %get-tuple-element.450), channel_id=1, source_target_pairs={{0,4},{4,8},{8,12},{12,0},{1,5},{5,9},{9,13},{13,1},{2,6},{6,10},{... | collective-permute-start | bytes 196616 | tf_op jit(solution)/shard_map/while/body/eval_jaxpr/ppermute | solution.py:19
  128.1 1.0 copy-start.4
  128.1 11.4 %copy-start.3 = (bf16[64,2048]{1,0:T(8,128)(2,1)S(1)}, bf16[64,2048]{1,0:T(8,128)(2,1)}, u32[]{:S(2)}) copy-start(bf16[64,2048]{1,0:T(8,128)(2,1)} %get-tuple-element.342) | copy-start | bytes 786436
  128.9 11.6 %copy-start.1 = (bf16[16,8,16,128]{3,1,2,0:T(8,128)(2,1)}, bf16[16,8,16,128]{3,1,2,0:T(8,128)(2,1)S(1)}, u32[]{:S(2)}) copy-start(bf16[16,8,16,128]{3,1,2,0:T(8,128)(2,1)S(1)} %copy.62) | copy-start | bytes 1572868
Sparse Core Ops, SparseCore 0:
  18.5 74.1 all-reduce.2
